TPU v7x, 256 devices: a whole 4x4x8 slice. The times are simulated.
256 devices in a mesh: grp: 32 (over x, y, core), blk: 8 (over z).
Axes of the slice: x: 4, y: 4, z: 8, core: 2. Of those that a mesh axis runs over, the one named last changes fastest.
Arguments:
- tiles_near: bfloat16 [16384, 256, 256], P(('grp', 'blk')), may hold values from -0.078125 to 0.078125
- near_cols: int32 [256, 64], P(('grp', 'blk')), may hold values from 0 to 3
- tiles_far: bfloat16 [6144, 256, 256], P(('grp', 'blk')), may hold values from -0.078125 to 0.078125
- far_groups: int32 [256, 24], P(('grp', 'blk')), may hold values from 0 to 31, as said below
- need_blocks: int32 [256, 32], P(('grp', 'blk')), may hold values from -1 to 3, as said below
- start_vectors: bfloat16 [262144, 128], P(('grp', 'blk')), may hold values from -6 to 6
Outputs:
- vectors: float32 [262144, 128], P(('grp', 'blk'))
Inputs may be any that keep to these rules, and one draw needn't show every extreme that they name: need_blocks[d, h] is -1 for d's own group and for groups d reads nothing from, else a row block index below 4 of the device of group h at d's position along blk; every device reads from at least one other group. far_groups[d, t] is a group h with need_blocks[d, h] >= 0.
All inputs are finite; a program needn't handle non-finite values.
Results may differ from a plain program's by a relative error of at most 0.0029.
Values may be sent and summed in bfloat16 or wider, within the bound.
A program may use at most 128 MiB of HBM per device.

v0:
```python
import jax
import jax.numpy as jnp
from jax import lax
from jax.sharding import PartitionSpec as P

ITERS = 2


def per_device(tiles_near, near_cols, tiles_far, far_groups, need_blocks, start_vectors):
    tile_size = tiles_near.shape[1]
    vec_width = start_vectors.shape[1]
    blocks = start_vectors.shape[0] // tile_size
    group_size = lax.axis_size("blk")
    group_count = lax.axis_size("grp")
    per_source = tiles_near.shape[0] // (blocks * group_size)
    far_each = tiles_far.shape[0] // blocks
    near_tiles = tiles_near.reshape(blocks, group_size, per_source, tile_size, tile_size)
    near_index = near_cols.reshape(blocks, group_size, per_source)
    far_tiles = tiles_far.reshape(blocks, far_each, tile_size, tile_size)
    far_index = far_groups.reshape(blocks, far_each)
    wanted = need_blocks.reshape(group_count)
    total_rows = blocks * tile_size * group_size * group_count
    current = start_vectors
    vectors = start_vectors.astype(jnp.float32)
    for iteration in range(ITERS):
        local_rows = current.reshape(blocks, tile_size, vec_width)
        group_table = lax.all_gather(local_rows, "blk", axis=0, tiled=True)
        source_ids = jnp.arange(group_size, dtype=jnp.int32)[None, :, None]
        chosen = group_table[source_ids * blocks + near_index]
        near_part = jnp.einsum(
            "rmnij,rmnjk->rik", near_tiles, chosen, preferred_element_type=jnp.float32
        )
        everything = lax.all_gather(local_rows, "grp", axis=0, tiled=True)
        far_rows = everything[far_index * blocks + wanted[far_index]]
        far_part = jnp.einsum(
            "rnij,rnjk->rik", far_tiles, far_rows, preferred_element_type=jnp.float32
        )
        product = near_part + far_part
        flat_rows = product.reshape(blocks * tile_size, vec_width)
        local_gram = jnp.dot(
            flat_rows.T,
            flat_rows,
            precision=lax.Precision.HIGHEST,
            preferred_element_type=jnp.float32,
        )
        gram = lax.psum(local_gram, ("grp", "blk")) / total_rows
        factor = jnp.linalg.cholesky(gram)
        identity_matrix = jnp.eye(vec_width, dtype=jnp.float32)
        inverse = lax.linalg.triangular_solve(factor, identity_matrix, left_side=True, lower=True).T
        vectors = jnp.dot(
            flat_rows, inverse, precision=lax.Precision.HIGHEST, preferred_element_type=jnp.float32
        )
        current = vectors.astype(jnp.bfloat16)
    return vectors


def solution(mesh):
    in_specs = (
        P(("grp", "blk"), None, None),
        P(("grp", "blk"), None),
        P(("grp", "blk"), None, None),
        P(("grp", "blk"), None),
        P(("grp", "blk"), None),
        P(("grp", "blk"), None),
    )
    out_specs = P(("grp", "blk"), None)
    return jax.shard_map(
        per_device, mesh=mesh, in_specs=in_specs, out_specs=out_specs, check_vma=False
    )
```

profile of v0, /device:TPU:1, one launch (start us, length us, event | category | flops | bytes accessed | tf_op | source)
XLA Modules:
  0.0 777.3 jit_solution(7489281376360508679)
XLA Ops:
  6.5 0.7 all-gather.5.cloned.1.call-update
  7.3 0.7 all-gather.7.cloned.1.call-update
  8.1 0.5 broadcast.166
  8.6 1.3 reduce.10
  10.1 1.4 gather_fusion.1
  11.6 1.3 reduce.11
  12.9 0.1 reshape.117
  13.1 0.1 reshape.129
  13.3 37.1 %all-gather.5.cloned.1.call-done = bf16[32,256,128]{2,1,0:T(8,128)(2,1)} async-done(((bf16[4,256,128]{2,1,0:T(8,128)(2,1)}), bf16[32,256,128]{2,1,0:T(8,128)(2,1)}) %all-gather.5.cloned.1.call-update) | async-done | bytes 2097168 | tf_op jit(solution)/shard_map/all_gather | solution.py:27
  50.4 4.6 gather_fusion
  55.0 58.5 %all-gather.7.cloned.1.call-done = bf16[128,256,128]{2,1,0:T(8,128)(2,1)} async-done(((bf16[4,256,128]{2,1,0:T(8,128)(2,1)}), bf16[128,256,128]{2,1,0:T(8,128)(2,1)}) %all-gather.7.cloned.1.call-update) | async-done | bytes 8388624 | tf_op jit(solution)/shard_map/all_gather | solution.py:33
  113.6 5.4 gather_fusion.2
  118.9 2.7 convolution_bitcast_fusion.1
  121.7 5.2 fusion.31
  126.9 0.8 copy-done.1
  127.7 1.2 convolution_bitcast_fusion.3
  129.0 2.0 copy.32
  131.0 235.3 %all-reduce.3.cloned.1.call-done = f32[128,128]{0,1:T(8,128)} async-done(((f32[128,128]{0,1:T(8,128)}), f32[128,128]{0,1:T(8,128)}) %all-reduce.3.cloned.1.call-update) | async-done | bytes 65552 | tf_op jit(solution)/shard_map/psum | solution.py:46
  366.3 0.8 broadcast_multiply_fusion.1
  367.2 0.1 copy.35
  367.3 0.9 fusion.45
  368.1 11.7 %cholesky.44 = f32[128,128]{1,0:T(8,128)S(1)} custom-call(f32[128,128]{1,0:T(8,128)S(1)} %fusion.45), custom_call_target="Cholesky" | custom-call | tf_op jit(solution)/shard_map/jit(cholesky)/cholesky | solution.py:47
  379.9 0.6 compare_reduce_fusion.1
  380.5 0.7 fusion.40
  381.2 9.8 %custom-call.6 = f32[1,128,128]{1,2,0:T(8,128)S(1)} custom-call(f32[1,128,128]{2,1,0:T(8,128)S(1)} %fusion.40), custom_call_target="InvertDiagBlocksLowerTriangular" | custom-call | tf_op jit(solution)/shard_map/triangular_solve/custom-call.0 | solution.py:49
  391.0 0.3 fusion.38
  391.3 2.3 convolution_convert_fusion
  393.7 0.5 all-gather.11.cloned.1.call-update
  394.2 0.2 all-reduce.5.cloned.1.call-start
  394.5 32.8 %all-gather.9.cloned.1.call-done = bf16[32,256,128]{2,1,0:T(8,128)(2,1)} async-done(((bf16[4,256,128]{2,1,0:T(8,128)(2,1)}), bf16[32,256,128]{2,1,0:T(8,128)(2,1)}) %all-gather.9.cloned.1.call-update) | async-done | bytes 2097168 | tf_op jit(solution)/shard_map/all_gather | solution.py:27
  427.3 4.6 gather_fusion.3
  432.0 58.4 %all-gather.11.cloned.1.call-done = bf16[128,256,128]{2,1,0:T(8,128)(2,1)} async-done(((bf16[4,256,128]{2,1,0:T(8,128)(2,1)}), bf16[128,256,128]{2,1,0:T(8,128)(2,1)}) %all-gather.11.cloned.1.call-update) | async-done | bytes 8388624 | tf_op jit(solution)/shard_map/all_gather | solution.py:33
  490.3 5.4 gather_fusion.4
  495.7 2.7 convolution_bitcast_fusion
  498.4 5.2 fusion.21
  503.7 0.8 copy-done.2
  504.5 1.2 convolution_bitcast_fusion.2
  505.7 2.0 copy.39
  507.7 235.3 %all-reduce.5.cloned.1.call-done = f32[128,128]{0,1:T(8,128)} async-done(((f32[128,128]{0,1:T(8,128)}), f32[128,128]{0,1:T(8,128)}) %all-reduce.5.cloned.1.call-update) | async-done | bytes 65552 | tf_op jit(solution)/shard_map/psum | solution.py:46
  743.1 0.8 broadcast_multiply_fusion
  743.9 0.1 copy.42
  744.0 0.9 fusion.43
  744.9 11.7 %cholesky.55 = f32[128,128]{1,0:T(8,128)S(1)} custom-call(f32[128,128]{1,0:T(8,128)S(1)} %fusion.43), custom_call_target="Cholesky" | custom-call | tf_op jit(solution)/shard_map/jit(cholesky)/cholesky | solution.py:47
  756.6 0.6 compare_reduce_fusion
  757.2 0.7 fusion.41
  757.9 9.8 %custom-call.7 = f32[1,128,128]{1,2,0:T(8,128)S(1)} custom-call(f32[1,128,128]{2,1,0:T(8,128)S(1)} %fusion.41), custom_call_target="InvertDiagBlocksLowerTriangular" | custom-call | tf_op jit(solution)/shard_map/triangular_solve/custom-call.0 | solution.py:49
  767.7 0.3 fusion.36
  768.0 2.4 fusion.46
  (29 shorter events, 0.8 us)
Async XLA Ops:
  6.5 112.4 %copy-start = (bf16[24,256,256]{2,1,0:T(8,128)(2,1)S(1)}, bf16[24,256,256]{2,1,0:T(8,128)(2,1)}, u32[]{:S(2)}) copy-start(bf16[24,256,256]{2,1,0:T(8,128)(2,1)} %param.11) | copy-start | bytes 9437188
  6.5 43.8 %all-gather.5.cloned.1.call-start = ((), (), s32[]{:S(2)}) async-start(), calls=%async_computation | async-start | bytes 2359296 | tf_op jit(solution)/shard_map/all_gather | solution.py:27
  7.3 106.3 %all-gather.7.cloned.1.call-start = ((), (), s32[]{:S(2)}) async-start(), calls=%async_computation.1 | async-start | bytes 8650752 | tf_op jit(solution)/shard_map/all_gather | solution.py:33
  8.0 358.3 %all-reduce.3.cloned.1.call-start = ((), (), s32[]{:S(2)}) async-start(), calls=%async_computation.2 | async-start | bytes 131072 | tf_op jit(solution)/shard_map/psum | solution.py:46
  118.9 2.7 copy-start.4
  126.9 0.8 copy-start.1
  128.9 298.4 %all-gather.9.cloned.1.call-start = ((), (), s32[]{:S(2)}) async-start(), calls=%async_computation.3 | async-start | bytes 2359296 | tf_op jit(solution)/shard_map/all_gather | solution.py:27
  393.6 96.7 %all-gather.11.cloned.1.call-start = ((), (), s32[]{:S(2)}) async-start(), calls=%async_computation.4 | async-start | bytes 8650752 | tf_op jit(solution)/shard_map/all_gather | solution.py:33
  394.2 348.8 %all-reduce.5.cloned.1.call-start = ((), (), s32[]{:S(2)}) async-start(), calls=%async_computation.5 | async-start | bytes 131072 | tf_op jit(solution)/shard_map/psum | solution.py:46
  495.7 2.7 copy-start.3
  503.7 0.8 copy-start.2
Sparse Core Ops, SparseCore 0:
  9.1 41.1 all-gather.4
  52.9 60.5 all-gather.6
  129.1 237.2 all-reduce.2
  393.8 33.4 all-gather.8
  429.7 60.5 all-gather.10
  505.8 237.1 all-reduce.4
where the time goes:
time: 778 us; the launch traced here: 777 us
  waiting for transfers between devices  659 us (85%)
  other arithmetic  51.9 us (7%)
  local copies, waits for them, and re-layouts  28.3 us (4%)
  matrix products  23.6 us (3%)
  between operations  13.7 us (2%)
    psum x2, waiting for transfers between devices, per_device(): gram = lax.psum(local_gram, ('grp', 'blk')) / total_rows  471 us
    all_gather x2, waiting for transfers between devices, per_device(): everything = lax.all_gather(local_rows, 'grp', axis=0, tiled=True)  117 us
    all_gather x2, waiting for transfers between devices, per_device(): group_table = lax.all_gather(local_rows, 'blk', axis=0, tiled=True)  70 us
    another operation x6, other arithmetic, per_device(): factor = jnp.linalg.cholesky(gram)  24.8 us
    another operation x4, other arithmetic, per_device(): lax.linalg.triangular_solve(factor, identity_matrix, left_side=True, lowe...  20.9 us
  transfers between devices with their start and end apart: 6, of which 6 were waited for; matrix products, arithmetic and copies ran while one was open for 2% of the time, Pallas kernels for 0%

commit v1 on v0

--- a/solution.py
+++ b/solution.py
@@ -24,7 +24,10 @@
     vectors = start_vectors.astype(jnp.float32)
     for iteration in range(ITERS):
         local_rows = current.reshape(blocks, tile_size, vec_width)
-        group_table = lax.all_gather(local_rows, "blk", axis=0, tiled=True)
+        size = lax.axis_size("blk")
+        pieces = jnp.stack([local_rows for _ in range(size)])
+        pieces = lax.all_to_all(pieces, "blk", split_axis=0, concat_axis=0)
+        group_table = jnp.concatenate(pieces, axis=0)
         source_ids = jnp.arange(group_size, dtype=jnp.int32)[None, :, None]
         chosen = group_table[source_ids * blocks + near_index]
         near_part = jnp.einsum(

time: 778 us -> 697 us (0.90)
  waiting for transfers between devices: 659 us -> 513 us
  blocking collectives: 0 us -> 54.4 us
  starting transfers between devices: 0.38 us -> 9.17 us
    all_gather x2, waiting for transfers between devices: 117 us -> 0.01 us  [per_device(): everything = lax.all_gather(local_rows, 'grp', axis=0, tiled=True)]
    all_gather x2 -> x0, waiting for transfers between devices: 70 us -> none  [per_device(): group_table = lax.all_gather(local_rows, 'blk', axis=0, tiled=True)]
    all_to_all x0 -> x1, blocking collectives: none -> 54.4 us  [per_device(): pieces = lax.all_to_all(pieces, 'blk', split_axis=0, concat_axis=0)]
    all_to_all x0 -> x1, waiting for transfers between devices: none -> 45.2 us  [per_device(): pieces = lax.all_to_all(pieces, 'blk', split_axis=0, concat_axis=0)]
    all_to_all x0 -> x1, starting transfers between devices: none -> 9.01 us  [per_device(): pieces = lax.all_to_all(pieces, 'blk', split_axis=0, concat_axis=0)]
  transfers between devices with their start and end apart: 6 -> 5, of which waited for: 6 -> 3; matrix products, arithmetic and copies ran while one was open for 2% -> 3% of each run, Pallas kernels for 0% -> 0%
where the time goes in v1:
time: 697 us; the launch traced here: 696 us
  waiting for transfers between devices  513 us (74%)
  blocking collectives  54.4 us (8%)
  other arithmetic  50.6 us (7%)
  local copies, waits for them, and re-layouts  32 us (5%)
  matrix products  23.6 us (3%)
  between operations  13.3 us (2%)
  starting transfers between devices  9.17 us (1%)
    psum x2, waiting for transfers between devices, per_device(): gram = lax.psum(local_gram, ('grp', 'blk')) / total_rows  467 us
    all_to_all x1, blocking collectives, per_device(): pieces = lax.all_to_all(pieces, 'blk', split_axis=0, concat_axis=0)  54.4 us
    all_to_all x1, waiting for transfers between devices, per_device(): pieces = lax.all_to_all(pieces, 'blk', split_axis=0, concat_axis=0)  45.2 us
    another operation x6, other arithmetic, per_device(): factor = jnp.linalg.cholesky(gram)  24.8 us
    another operation x4, other arithmetic, per_device(): lax.linalg.triangular_solve(factor, identity_matrix, left_side=True, lowe...  20.9 us
  transfers between devices with their start and end apart: 5, of which 3 were waited for; matrix products, arithmetic and copies ran while one was open for 3% of the time, Pallas kernels for 0%

profile of v1, /device:TPU:1, one launch (start us, length us, event | category | flops | bytes accessed | tf_op | source)
XLA Modules:
  0.0 695.9 jit_solution(209102806035530164)
XLA Ops:
  6.6 0.7 all-gather.3.cloned.1.call-update
  7.3 3.0 stack.6
  10.2 9.0 %all-to-all-start = ((bf16[8,4,256,128]{3,2,1,0:T(8,128)(2,1)}), bf16[8,4,256,128]{3,2,1,0:T(8,128)(2,1)}, u32[]{:S(2)}, u32[]{:S(2)}) async-start(bf16[8,4,256,128]{3,2,1,0:T(8,128)(2,1)} %stack.6), calls=%async_computation | async-start | bytes 4194304 | tf_op jit(solution)/shard_map/all_to_all | solution.py:29
  19.3 0.5 broadcast.168
  19.8 0.7 reduce.11
  20.5 0.7 reduce.10
  21.2 0.1 reshape.143
  21.3 0.7 gather_fusion.1
  22.1 0.1 reshape.151
  22.2 0.1 reshape.123
  22.4 0.1 reshape.135
  22.6 45.2 %all-to-all-done = bf16[8,4,256,128]{3,2,1,0:T(8,128)(2,1)} async-done(((bf16[8,4,256,128]{3,2,1,0:T(8,128)(2,1)}), bf16[8,4,256,128]{3,2,1,0:T(8,128)(2,1)}, u32[]{:S(2)}, u32[]{:S(2)}) %all-to-all-start) | async-done | bytes 2097184 | tf_op jit(solution)/shard_map/all_to_all | solution.py:29
  67.8 4.6 gather_fusion
  72.4 5.4 gather_fusion.2
  77.8 2.7 convolution_bitcast_fusion.1
  80.6 5.2 fusion.31
  85.8 0.8 copy-done.2
  86.6 1.2 convolution_bitcast_fusion.3
  87.9 2.0 copy.30
  89.9 235.6 %all-reduce.3.cloned.1.call-done = f32[128,128]{0,1:T(8,128)} async-done(((f32[128,128]{0,1:T(8,128)}), f32[128,128]{0,1:T(8,128)}) %all-reduce.3.cloned.1.call-update) | async-done | bytes 65552 | tf_op jit(solution)/shard_map/psum | solution.py:49
  325.5 0.8 broadcast_multiply_fusion.1
  326.4 0.1 copy.33
  326.5 0.9 fusion.45
  327.3 11.7 %cholesky.44 = f32[128,128]{1,0:T(8,128)S(1)} custom-call(f32[128,128]{1,0:T(8,128)S(1)} %fusion.45), custom_call_target="Cholesky" | custom-call | tf_op jit(solution)/shard_map/jit(cholesky)/cholesky | solution.py:50
  339.1 0.6 compare_reduce_fusion.1
  339.7 0.7 fusion.40
  340.4 9.8 %custom-call.6 = f32[1,128,128]{1,2,0:T(8,128)S(1)} custom-call(f32[1,128,128]{2,1,0:T(8,128)S(1)} %fusion.40), custom_call_target="InvertDiagBlocksLowerTriangular" | custom-call | tf_op jit(solution)/shard_map/triangular_solve/custom-call.0 | solution.py:52
  350.2 0.3 fusion.38
  350.5 2.3 convolution_convert_fusion
  352.9 1.4 stack.7
  354.3 54.4 %all_to_all.10 = bf16[8,4,256,128]{3,2,1,0:T(8,128)(2,1)} all-to-all(bf16[8,4,256,128]{3,2,1,0:T(8,128)(2,1)S(1)} %stack.7), channel_id=1, replica_groups=mesh['grp'=32,'blk'=8] {'blk'}, dimensions={0} | all-to-all | bytes 4194304 | tf_op jit(solution)/shard_map/all_to_all | solution.py:29
  408.7 4.6 gather_fusion.3
  413.3 5.4 gather_fusion.4
  418.7 2.7 convolution_bitcast_fusion
  421.5 5.2 fusion.21
  426.7 0.8 copy-done.3
  427.5 1.2 convolution_bitcast_fusion.2
  428.7 2.0 copy.37
  430.8 231.3 %all-reduce.5.cloned.1.call-done = f32[128,128]{0,1:T(8,128)} async-done(((f32[128,128]{0,1:T(8,128)}), f32[128,128]{0,1:T(8,128)}) %all-reduce.5.cloned.1.call-update) | async-done | bytes 65552 | tf_op jit(solution)/shard_map/psum | solution.py:49
  662.0 0.8 broadcast_multiply_fusion
  662.9 0.1 copy.40
  663.0 0.9 fusion.43
  663.8 11.7 %cholesky.55 = f32[128,128]{1,0:T(8,128)S(1)} custom-call(f32[128,128]{1,0:T(8,128)S(1)} %fusion.43), custom_call_target="Cholesky" | custom-call | tf_op jit(solution)/shard_map/jit(cholesky)/cholesky | solution.py:50
  675.6 0.6 compare_reduce_fusion
  676.2 0.7 fusion.41
  676.9 9.8 %custom-call.7 = f32[1,128,128]{1,2,0:T(8,128)S(1)} custom-call(f32[1,128,128]{2,1,0:T(8,128)S(1)} %fusion.41), custom_call_target="InvertDiagBlocksLowerTriangular" | custom-call | tf_op jit(solution)/shard_map/triangular_solve/custom-call.0 | solution.py:52
  686.7 0.3 fusion.36
  687.0 2.4 fusion.46
  (34 shorter events, 0.6 us)
Async XLA Ops:
  6.5 71.3 %copy-start = (bf16[24,256,256]{2,1,0:T(8,128)(2,1)S(1)}, bf16[24,256,256]{2,1,0:T(8,128)(2,1)}, u32[]{:S(2)}) copy-start(bf16[24,256,256]{2,1,0:T(8,128)(2,1)} %param.11) | copy-start | bytes 9437188
  6.5 13.3 %copy-start.6 = (s32[1,64]{1,0:T(1,128)S(1)}, s32[1,64]{1,0:T(1,128)}, u32[]{:S(2)}) copy-start(s32[1,64]{1,0:T(1,128)} %param.10) | copy-start | bytes 772
  6.5 13.9 %copy-start.7 = (s32[1,24]{1,0:T(1,128)S(1)}, s32[1,24]{1,0:T(1,128)}, u32[]{:S(2)}) copy-start(s32[1,24]{1,0:T(1,128)} %param.12) | copy-start | bytes 292
  6.5 14.8 %copy-start.1 = (s32[1,32]{1,0:T(1,128)S(1)}, s32[1,32]{1,0:T(1,128)}, u32[]{:S(2)}) copy-start(s32[1,32]{1,0:T(1,128)} %param.13) | copy-start | bytes 388
  6.5 65.9 %all-gather.3.cloned.1.call-start = ((), (), s32[]{:S(2)}) async-start(), calls=%async_computation.2 | async-start | bytes 8650752 | tf_op jit(solution)/shard_map/all_gather | solution.py:36
  10.2 57.5 %all-to-all-start = ((bf16[8,4,256,128]{3,2,1,0:T(8,128)(2,1)}), bf16[8,4,256,128]{3,2,1,0:T(8,128)(2,1)}, u32[]{:S(2)}, u32[]{:S(2)}) async-start(bf16[8,4,256,128]{3,2,1,0:T(8,128)(2,1)} %stack.6), calls=%async_computation | async-start | bytes 4194304 | tf_op jit(solution)/shard_map/all_to_all | solution.py:29
  19.2 306.3 %all-reduce.3.cloned.1.call-start = ((), (), s32[]{:S(2)}) async-start(), calls=%async_computation.3 | async-start | bytes 131072 | tf_op jit(solution)/shard_map/psum | solution.py:49
  77.8 2.7 copy-start.5
  85.8 0.8 copy-start.2
  87.8 325.5 %all-gather.5.cloned.1.call-start = ((), (), s32[]{:S(2)}) async-start(), calls=%async_computation.4 | async-start | bytes 8650752 | tf_op jit(solution)/shard_map/all_gather | solution.py:36
  352.8 309.2 %all-reduce.5.cloned.1.call-start = ((), (), s32[]{:S(2)}) async-start(), calls=%async_computation.5 | async-start | bytes 131072 | tf_op jit(solution)/shard_map/psum | solution.py:49
  418.7 2.7 copy-start.4
  426.7 0.8 copy-start.3
Sparse Core Ops, SparseCore 0:
  9.9 62.1 all-gather.2
  87.9 237.5 all-reduce.2
  353.0 54.4 all-gather.4
  428.8 233.1 all-reduce.4
